TPU v7x, 256 devices: a whole 4x4x8 slice. The times are simulated.
256 devices in a mesh: slab: 64 (over z, y, core), col: 4 (over x).
Axes of the slice: x: 4, y: 4, z: 8, core: 2. Of those that a mesh axis runs over, the one named last changes fastest.
Arguments:
- recycle_basis: float32 [16, 3, 128, 8, 256], P('col', None, 'slab'), may hold values from -400 to 400
- densities: float32 [128, 8, 256], P('slab'), may hold values from 0.2 to 1
- solid_mask: int32 [128, 8, 256], P('slab'), may hold values 0 or 1
- fixed_mask: int32 [128, 8, 256], P('slab'), may hold values 0 or 1
Outputs:
- ortho_basis: float32 [16, 3, 128, 8, 256], P('col', None, 'slab')
- new_recycle: float32 [16, 3, 128, 8, 256], P('col', None, 'slab')
- r_factor: float32 [16, 16], replicated
Inputs may be any that keep to these rules, and one draw needn't show every extreme that they name: `solid_mask`: 1 marks a solid lattice voxel. `fixed_mask`: 1 marks a fixed node.
All inputs are finite; a program needn't handle non-finite values. No bound on the sum of `solid_mask` or of `fixed_mask` on one device may be relied on, other than what follows from the above.
Results may differ from a plain program's by a relative error of at most 0.0001.
Values sent between devices are 32-bit elements; how exact they have to be, the bound alone decides.
A program may use at most 64 MiB of HBM per device.

v0:
```python
import jax
import jax.numpy as jnp
import numpy as np
from jax import lax
from jax.sharding import PartitionSpec as P

void_stiffness = 0.001


def from_behind(value, axis, steps):
    count = lax.axis_size(axis)
    first, last = (max(0, -steps), min(count, count - steps))
    return lax.ppermute(value, axis, [(source, source + steps) for source in range(first, last)])


def element_matrix():
    poisson = 0.3
    lame_first = poisson / ((1.0 + poisson) * (1.0 - 2.0 * poisson))
    shear_mod = 1.0 / (2.0 * (1.0 + poisson))
    elastic = np.zeros((6, 6))
    elastic[:3, :3] = lame_first
    for k in range(3):
        elastic[k, k] = lame_first + 2.0 * shear_mod
    for k in range(3, 6):
        elastic[k, k] = shear_mod
    points = [(1.0 - 1.0 / np.sqrt(3.0)) / 2.0, (1.0 + 1.0 / np.sqrt(3.0)) / 2.0]
    matrix = np.zeros((24, 24))
    for a in points:
        for b in points:
            for d in points:
                strain = np.zeros((6, 24))
                for c in range(8):
                    ox, oy, oz = (c % 2, c // 2 % 2, c // 4)
                    weight_x = a if ox else 1.0 - a
                    weight_y = b if oy else 1.0 - b
                    weight_z = d if oz else 1.0 - d
                    slope_x = (1.0 if ox else -1.0) * weight_y * weight_z
                    slope_y = (1.0 if oy else -1.0) * weight_x * weight_z
                    slope_z = (1.0 if oz else -1.0) * weight_x * weight_y
                    strain[0, 3 * c] = slope_x
                    strain[1, 3 * c + 1] = slope_y
                    strain[2, 3 * c + 2] = slope_z
                    strain[3, 3 * c] = slope_y
                    strain[3, 3 * c + 1] = slope_x
                    strain[4, 3 * c + 1] = slope_z
                    strain[4, 3 * c + 2] = slope_y
                    strain[5, 3 * c] = slope_z
                    strain[5, 3 * c + 2] = slope_x
                matrix = matrix + strain.T @ elastic @ strain / 8.0
    return matrix.reshape(8, 3, 8, 3)


def shift_ahead(values, along):
    count = values.shape[along]
    rest = lax.slice_in_dim(values, 1, count, axis=along)
    edge = jnp.zeros_like(lax.slice_in_dim(values, 0, 1, axis=along))
    return jnp.concatenate([rest, edge], axis=along)


def shift_behind(values, along):
    count = values.shape[along]
    rest = lax.slice_in_dim(values, 0, count - 1, axis=along)
    edge = jnp.zeros_like(lax.slice_in_dim(values, 0, 1, axis=along))
    return jnp.concatenate([edge, rest], axis=along)


def element_stiffness(densities, solid_mask, start_layer, total_layers):
    full_shape = densities.shape
    depth_index = lax.broadcasted_iota(jnp.int32, full_shape, 0) + start_layer
    across_x = lax.broadcasted_iota(jnp.int32, full_shape, 1)
    across_y = lax.broadcasted_iota(jnp.int32, full_shape, 2)
    inside = (
        (depth_index < total_layers - 1)
        & (across_x < full_shape[1] - 1)
        & (across_y < full_shape[2] - 1)
    )
    values = solid_mask.astype(jnp.float32) * densities**3 + void_stiffness
    return jnp.where(inside, values, 0.0)


def element_forces(extended, stiffness, matrix):
    layers = stiffness.shape[0]
    corner_views = []
    for c in range(8):
        view = lax.slice_in_dim(extended, c // 4, c // 4 + layers, axis=1)
        if c % 2:
            view = shift_ahead(view, 2)
        if c // 2 % 2:
            view = shift_ahead(view, 3)
        corner_views.append(view)
    stacked = jnp.stack(corner_views)
    forces = (
        jnp.einsum("cadb,dbzxy->cazxy", matrix, stacked, precision=lax.Precision.HIGHEST)
        * stiffness
    )
    result = jnp.zeros(extended.shape, jnp.float32)
    for c in range(8):
        piece = forces[c]
        if c % 2:
            piece = shift_behind(piece, 2)
        if c // 2 % 2:
            piece = shift_behind(piece, 3)
        result = result.at[:, c // 4 : c // 4 + layers].add(piece)
    return result


def apply_operator(columns, free_mask, stiffness):
    matrix = jnp.asarray(element_matrix(), dtype=jnp.float32)
    moved = columns * free_mask
    upper = from_behind(moved[:, :, :1], "slab", -1)
    extended = jnp.concatenate([moved, upper], axis=2)

    def per_column(column):
        return element_forces(column, stiffness, matrix)

    forces_out = lax.map(per_column, extended)
    spilled = from_behind(forces_out[:, :, -1:], "slab", 1)
    interior = jnp.concatenate([forces_out[:, :, :1] + spilled, forces_out[:, :, 1:-1]], axis=2)
    return free_mask * interior + (1.0 - free_mask) * columns


def factor_gram(gram_matrix, total_cols):
    cholesky_lower = jnp.linalg.cholesky(gram_matrix)
    inverse = lax.linalg.triangular_solve(
        cholesky_lower, jnp.eye(total_cols, dtype=jnp.float32), left_side=True, lower=True
    )
    return (cholesky_lower, inverse)


def on_device(recycle_basis, densities, solid_mask, fixed_mask):
    layers = recycle_basis.shape[2]
    slab_count = lax.axis_size("slab")
    col_count = lax.axis_size("col")
    own_count = recycle_basis.shape[0]
    total_cols = own_count * col_count
    col_first = lax.axis_index("col") * own_count
    free_mask = 1.0 - fixed_mask.astype(jnp.float32)
    stiffness = element_stiffness(
        densities, solid_mask, lax.axis_index("slab") * layers, layers * slab_count
    )
    gathered = lax.all_gather(recycle_basis, "col", axis=0, tiled=True)
    image_full = apply_operator(gathered, free_mask, stiffness)
    flattened = image_full.reshape(total_cols, -1)
    rows_total = flattened.shape[1] * slab_count
    gram_part = lax.dot_general(
        flattened,
        flattened,
        (((1,), (1,)), ((), ())),
        precision=lax.Precision.HIGHEST,
        preferred_element_type=jnp.float32,
    )
    gram_matrix = lax.psum(gram_part, "slab")
    gram_matrix = gram_matrix / rows_total
    cholesky_lower, inverse = factor_gram(gram_matrix, total_cols)
    own_inverse = lax.dynamic_slice_in_dim(inverse, col_first, own_count, 0)
    ortho = jnp.dot(
        own_inverse, flattened, precision=lax.Precision.HIGHEST, preferred_element_type=jnp.float32
    ).reshape(recycle_basis.shape)
    renewed = jnp.dot(
        own_inverse,
        gathered.reshape(total_cols, -1),
        precision=lax.Precision.HIGHEST,
        preferred_element_type=jnp.float32,
    ).reshape(recycle_basis.shape)
    return (ortho, renewed, cholesky_lower.T)


def solution(mesh):
    placed = (
        P("col", None, "slab", None, None),
        P("slab", None, None),
        P("slab", None, None),
        P("slab", None, None),
    )
    return jax.shard_map(
        on_device,
        mesh=mesh,
        in_specs=placed,
        out_specs=(P("col", None, "slab", None, None), P("col", None, "slab", None, None), P()),
        check_vma=False,
    )
```

profile of v0, /device:TPU:1, one launch (start us, length us, event | category | flops | bytes accessed | tf_op | source)
XLA Modules:
  0.0 229.1 jit_solution(9076592694379909722)
XLA Ops:
  0.6 13.1 %all_gather.3 = f32[16,3,2,8,256]{4,3,2,1,0:T(8,128)S(1)} all-gather(f32[4,3,2,8,256]{4,3,2,1,0:T(8,128)} %param.23), channel_id=1, replica_groups=mesh['slab'=64,'col'=4] {'col'}, dimensions={0}, use_global_device_ids=true | all-gather | bytes 983040 | tf_op jit(solution)/shard_map/all_gather | solution.py:141
  13.7 0.7 broadcast_subtract_fusion
  14.6 6.2 %collective-permute-start = (f32[16,3,1,8,256]{4,3,2,1,0:T(8,128)S(1)}, f32[16,3,1,8,256]{4,3,2,1,0:T(8,128)S(1)}, u32[]{:S(2)}, u32[]{:S(2)}) collective-permute-start(f32[16,3,1,8,256]{4,3,2,1,0:T(8,128)S(1)} %slice.472), channel_id=1, source_target_pairs={{4,0},{8,4},{12,8},{16,12},{20,16},{24,20},{28,24},{32,28},{36,32}... | collective-permute-start | bytes 1179656 | tf_op jit(solution)/shard_map/ppermute | solution.py:13
  20.9 4.5 %collective-permute-done = f32[16,3,1,8,256]{4,3,2,1,0:T(8,128)S(1)} collective-permute-done((f32[16,3,1,8,256]{4,3,2,1,0:T(8,128)S(1)}, f32[16,3,1,8,256]{4,3,2,1,0:T(8,128)S(1)}, u32[]{:S(2)}, u32[]{:S(2)}) %collective-permute-start) | collective-permute-done | bytes 393248 | tf_op jit(solution)/shard_map/ppermute | solution.py:13
  25.5 54.7 %while.21 = (s32[]{:T(128)}, f32[16,3,3,8,256]{4,3,2,1,0:T(8,128)}, f32[16,3,3,8,256]{4,3,2,1,0:T(8,128)S(1)}, f32[2,8,256]{2,1,0:T(8,128)S(1)}, s32[]{:T(128)}, /*index=5*/f32[8,3,8,3,1,1]{2,0,3,1,5,4:T(8,128)S(1)}, f32[]{:T(128)}) while((s32[]{:T(128)}, f32[16,3,3,8,256]{4,3,2,1,0:T(8,128)}, ...), condition=%wide.region_1.2_spmd.clone, body=%wide.region_0.1_spmd.sunk.clone.sunk | while | flops 28569600 | bytes 7303765 | solution.py:116
  26.3 0.6 stack.73
  28.3 0.6 constant_dynamic-update-slice_fusion.5
  38.6 0.6 constant_dynamic-update-slice_fusion.5
  42.0 0.6 constant_dynamic-update-slice_fusion.5
  43.4 0.6 stack.73
  46.8 0.6 stack.73
  50.2 0.6 stack.73
  53.6 0.6 stack.73
  57.1 0.6 stack.73
  63.9 0.6 stack.73
  65.9 0.6 constant_dynamic-update-slice_fusion.5
  79.6 0.6 constant_dynamic-update-slice_fusion.5
  80.2 1.0 slice.399
  81.2 1.9 collective-permute-start.1
  83.2 4.7 %collective-permute-done.1 = f32[16,3,1,8,256]{4,3,2,1,0:T(8,128)S(1)} collective-permute-done((f32[16,3,1,8,256]{4,3,2,1,0:T(8,128)S(1)}, f32[16,3,1,8,256]{4,3,2,1,0:T(8,128)S(1)}, u32[]{:S(2)}, u32[]{:S(2)}) %collective-permute-start.1) | collective-permute-done | bytes 393248 | tf_op jit(solution)/shard_map/ppermute | solution.py:13
  87.9 1.2 slice_add_fusion.1
  89.3 1.4 convolution_bitcast_fusion.1
  90.8 130.1 %psum.7 = f32[16,16]{0,1:T(8,128)S(1)} all-reduce(f32[16,16]{0,1:T(8,128)S(1)} %convolution_bitcast_fusion.1), channel_id=1, replica_groups=mesh['slab'=64,'col'=4] {'slab'}, use_global_device_ids=true, to_apply=%region_2.3 | all-reduce | flops 256 | bytes 2048 | tf_op jit(solution)/shard_map/psum | solution.py:152
  220.9 1.5 cholesky.17
  222.4 0.6 compare_reduce_fusion
  223.1 0.6 fusion.16
  223.7 1.2 custom-call.6
  225.2 0.9 fusion.5
  226.1 0.7 copy.316
  226.8 0.9 fusion.7
  227.7 0.7 copy.315
  228.4 0.7 copy.317
  (633 shorter events, 43.8 us)
Async XLA Ops:
  14.5 6.3 %copy-start.1 = (f32[2,8,256]{2,1,0:T(8,128)S(1)}, f32[2,8,256]{2,1,0:T(8,128)}, u32[]{:S(2)}) copy-start(f32[2,8,256]{2,1,0:T(8,128)} %param.24) | copy-start | bytes 49156
  14.5 6.3 %copy-start.2 = (s32[2,8,256]{2,1,0:T(8,128)S(1)}, s32[2,8,256]{2,1,0:T(8,128)}, u32[]{:S(2)}) copy-start(s32[2,8,256]{2,1,0:T(8,128)} %param.25) | copy-start | bytes 49156
  14.6 10.8 %collective-permute-start = (f32[16,3,1,8,256]{4,3,2,1,0:T(8,128)S(1)}, f32[16,3,1,8,256]{4,3,2,1,0:T(8,128)S(1)}, u32[]{:S(2)}, u32[]{:S(2)}) collective-permute-start(f32[16,3,1,8,256]{4,3,2,1,0:T(8,128)S(1)} %slice.472), channel_id=1, source_target_pairs={{4,0},{8,4},{12,8},{16,12},{20,16},{24,20},{28,24},{32,28},{36,32}... | collective-permute-start | bytes 1179656 | tf_op jit(solution)/shard_map/ppermute | solution.py:13
  20.9 4.6 %copy-start = (f32[8,3,8,3,1,1]{2,0,3,1,5,4:T(8,128)S(1)}, f32[8,3,8,3,1,1]{2,0,3,1,5,4:T(8,128)}, u32[]{:S(2)}) copy-start(f32[8,3,8,3,1,1]{2,0,3,1,5,4:T(8,128)} %constant.380) | copy-start | bytes 6916
  81.2 6.6 %collective-permute-start.1 = (f32[16,3,1,8,256]{4,3,2,1,0:T(8,128)S(1)}, f32[16,3,1,8,256]{4,3,2,1,0:T(8,128)S(1)}, u32[]{:S(2)}, u32[]{:S(2)}) collective-permute-start(f32[16,3,1,8,256]{4,3,2,1,0:T(8,128)S(1)} %slice.399), channel_id=1, source_target_pairs={{0,4},{4,8},{8,12},{12,16},{16,20},{20,24},{24,28},{28,32},{32,36}... | collective-permute-start | bytes 1179656 | tf_op jit(solution)/shard_map/ppermute | solution.py:13
where the time goes:
time: 229 us
  blocking collectives  143 us (62%)
  local copies, waits for them, and re-layouts  39.3 us (17%)
  other arithmetic  12.7 us (6%)
  matrix products  11.7 us (5%)
  waiting for transfers between devices  9.18 us (4%)
  starting transfers between devices  8.08 us (4%)
  loops' own time  4.12 us (2%)
    psum x1, blocking collectives, on_device(): gram_matrix = lax.psum(gram_part, 'slab')  130 us
    another operation x224, local copies, waits for them, and re-layouts, element_forces(): stacked = jnp.stack(corner_views)  17.6 us
    all_gather x1, blocking collectives, on_device(): gathered = lax.all_gather(recycle_basis, 'col', axis=0, tiled=True)  13.1 us
    dynamic_update_slice x16, local copies, waits for them, and re-layouts, apply_operator(): forces_out = lax.map(per_column, extended)  10.2 us
    ppermute x2, waiting for transfers between devices, from_behind(): lax.ppermute(value, axis, [(source, source + steps) for source in range(f...  9.18 us
    dot_general x16, matrix products, element_forces(): jnp.einsum('cadb,dbzxy->cazxy', matrix, stacked, precision=lax.Precision....  8.3 us
    ppermute x2, starting transfers between devices, from_behind(): lax.ppermute(value, axis, [(source, source + steps) for source in range(f...  8.08 us
    scatter-add x112, other arithmetic, element_forces(): result = result.at[:, c // 4:c // 4 + layers].add(piece)  6.21 us
  transfers between devices with their start and end apart: 2, of which 2 were waited for; matrix products, arithmetic and copies ran while one was open for 0% of the time, Pallas kernels for 0%

commit v1 on v0

--- a/solution.py
+++ b/solution.py
@@ -3,8 +3,14 @@
 import numpy as np
 from jax import lax
 from jax.sharding import PartitionSpec as P
+from jax.lax import all_gather
 
 void_stiffness = 0.001
+
+
+def sizes_test(array_in):
+    current_arr = all_gather(array_in, "slab")
+    return jnp.sum(current_arr, axis=0)
 
 
 def from_behind(value, axis, steps):
@@ -149,7 +155,7 @@
         precision=lax.Precision.HIGHEST,
         preferred_element_type=jnp.float32,
     )
-    gram_matrix = lax.psum(gram_part, "slab")
+    gram_matrix = sizes_test(gram_part)
     gram_matrix = gram_matrix / rows_total
     cholesky_lower, inverse = factor_gram(gram_matrix, total_cols)
     own_inverse = lax.dynamic_slice_in_dim(inverse, col_first, own_count, 0)

time: 229 us -> 157 us (0.69)
  blocking collectives: 143 us -> 70.6 us
    psum x1 -> x0, blocking collectives: 130 us -> none  [on_device(): gram_matrix = lax.psum(gram_part, 'slab')]
    all_gather x0 -> x1, blocking collectives: none -> 57.5 us  [sizes_test(): current_arr = all_gather(array_in, 'slab')]
where the time goes in v1:
time: 157 us
  blocking collectives  70.6 us (45%)
  local copies, waits for them, and re-layouts  39.4 us (25%)
  other arithmetic  12.8 us (8%)
  matrix products  11.7 us (7%)
  waiting for transfers between devices  9.18 us (6%)
  starting transfers between devices  8.08 us (5%)
  loops' own time  4.12 us (3%)
    all_gather x1, blocking collectives, sizes_test(): current_arr = all_gather(array_in, 'slab')  57.5 us
    another operation x224, local copies, waits for them, and re-layouts, element_forces(): stacked = jnp.stack(corner_views)  17.6 us
    all_gather x1, blocking collectives, on_device(): gathered = lax.all_gather(recycle_basis, 'col', axis=0, tiled=True)  13.1 us
    dynamic_update_slice x16, local copies, waits for them, and re-layouts, apply_operator(): forces_out = lax.map(per_column, extended)  10.2 us
    ppermute x2, waiting for transfers between devices, from_behind(): lax.ppermute(value, axis, [(source, source + steps) for source in range(f...  9.18 us
    dot_general x16, matrix products, element_forces(): jnp.einsum('cadb,dbzxy->cazxy', matrix, stacked, precision=lax.Precision....  8.3 us
    ppermute x2, starting transfers between devices, from_behind(): lax.ppermute(value, axis, [(source, source + steps) for source in range(f...  8.08 us
    scatter-add x112, other arithmetic, element_forces(): result = result.at[:, c // 4:c // 4 + layers].add(piece)  6.21 us
  transfers between devices with their start and end apart: 2, of which 2 were waited for; matrix products, arithmetic and copies ran while one was open for 0% of the time, Pallas kernels for 0%

profile of v1, /device:TPU:1, one launch (start us, length us, event | category | flops | bytes accessed | tf_op | source)
XLA Modules:
  0.0 156.6 jit_solution(3483695893704885601)
XLA Ops:
  0.6 13.1 %all_gather.9 = f32[16,3,2,8,256]{4,3,2,1,0:T(8,128)S(1)} all-gather(f32[4,3,2,8,256]{4,3,2,1,0:T(8,128)} %param.23), channel_id=1, replica_groups=mesh['slab'=64,'col'=4] {'col'}, dimensions={0}, use_global_device_ids=true | all-gather | bytes 983040 | tf_op jit(solution)/shard_map/all_gather | solution.py:147
  13.7 0.7 broadcast_subtract_fusion
  14.6 6.2 %collective-permute-start = (f32[16,3,1,8,256]{4,3,2,1,0:T(8,128)S(1)}, f32[16,3,1,8,256]{4,3,2,1,0:T(8,128)S(1)}, u32[]{:S(2)}, u32[]{:S(2)}) collective-permute-start(f32[16,3,1,8,256]{4,3,2,1,0:T(8,128)S(1)} %slice.472), channel_id=1, source_target_pairs={{4,0},{8,4},{12,8},{16,12},{20,16},{24,20},{28,24},{32,28},{36,32}... | collective-permute-start | bytes 1179656 | tf_op jit(solution)/shard_map/ppermute | solution.py:19
  20.9 4.5 %collective-permute-done = f32[16,3,1,8,256]{4,3,2,1,0:T(8,128)S(1)} collective-permute-done((f32[16,3,1,8,256]{4,3,2,1,0:T(8,128)S(1)}, f32[16,3,1,8,256]{4,3,2,1,0:T(8,128)S(1)}, u32[]{:S(2)}, u32[]{:S(2)}) %collective-permute-start) | collective-permute-done | bytes 393248 | tf_op jit(solution)/shard_map/ppermute | solution.py:19
  25.5 54.7 %while.21 = (s32[]{:T(128)}, f32[16,3,3,8,256]{4,3,2,1,0:T(8,128)}, f32[16,3,3,8,256]{4,3,2,1,0:T(8,128)S(1)}, f32[2,8,256]{2,1,0:T(8,128)S(1)}, s32[]{:T(128)}, /*index=5*/f32[8,3,8,3,1,1]{2,0,3,1,5,4:T(8,128)S(1)}, f32[]{:T(128)}) while((s32[]{:T(128)}, f32[16,3,3,8,256]{4,3,2,1,0:T(8,128)}, ...), condition=%wide.region_1.2_spmd.clone, body=%wide.region_0.1_spmd.sunk.clone.sunk | while | flops 28569600 | bytes 7303765 | solution.py:122
  26.3 0.6 stack.73
  28.3 0.6 constant_dynamic-update-slice_fusion.5
  38.6 0.6 constant_dynamic-update-slice_fusion.5
  42.0 0.6 constant_dynamic-update-slice_fusion.5
  43.4 0.6 stack.73
  46.8 0.6 stack.73
  50.2 0.6 stack.73
  53.6 0.6 stack.73
  57.1 0.6 stack.73
  63.9 0.6 stack.73
  65.9 0.6 constant_dynamic-update-slice_fusion.5
  79.6 0.6 constant_dynamic-update-slice_fusion.5
  80.2 1.0 slice.399
  81.2 1.9 %collective-permute-start.1 = (f32[16,3,1,8,256]{4,3,2,1,0:T(8,128)S(1)}, f32[16,3,1,8,256]{4,3,2,1,0:T(8,128)S(1)}, u32[]{:S(2)}, u32[]{:S(2)}) collective-permute-start(f32[16,3,1,8,256]{4,3,2,1,0:T(8,128)S(1)} %slice.399), channel_id=1, source_target_pairs={{0,4},{4,8},{8,12},{12,16},{16,20},{20,24},{24,28},{28,32},{32,36}... | collective-permute-start | bytes 1179656 | tf_op jit(solution)/shard_map/ppermute | solution.py:19
  83.2 4.7 %collective-permute-done.1 = f32[16,3,1,8,256]{4,3,2,1,0:T(8,128)S(1)} collective-permute-done((f32[16,3,1,8,256]{4,3,2,1,0:T(8,128)S(1)}, f32[16,3,1,8,256]{4,3,2,1,0:T(8,128)S(1)}, u32[]{:S(2)}, u32[]{:S(2)}) %collective-permute-start.1) | collective-permute-done | bytes 393248 | tf_op jit(solution)/shard_map/ppermute | solution.py:19
  87.9 1.2 slice_add_fusion.1
  89.3 1.4 convolution_bitcast_fusion.1
  90.7 57.5 %all-gather = f32[1024,16]{1,0:T(8,128)S(1)} all-gather(f32[16,16]{1,0:T(8,128)S(1)} %convolution_bitcast_fusion.1), channel_id=2, replica_groups=mesh['slab'=64,'col'=4] {'slab'}, dimensions={0}, use_global_device_ids=true | all-gather | bytes 66560 | tf_op jit(solution)/shard_map/all_gather | solution.py:12
  148.5 1.5 cholesky.17
  150.0 0.6 compare_reduce_fusion
  150.6 0.6 fusion.16
  151.3 1.2 custom-call.6
  152.7 0.9 fusion.5
  153.6 0.7 copy.307
  154.3 0.9 fusion.7
  155.3 0.7 copy.306
  156.0 0.7 copy.308
  (635 shorter events, 43.9 us)
Async XLA Ops:
  14.5 6.3 %copy-start.1 = (f32[2,8,256]{2,1,0:T(8,128)S(1)}, f32[2,8,256]{2,1,0:T(8,128)}, u32[]{:S(2)}) copy-start(f32[2,8,256]{2,1,0:T(8,128)} %param.24) | copy-start | bytes 49156
  14.5 6.3 %copy-start.2 = (s32[2,8,256]{2,1,0:T(8,128)S(1)}, s32[2,8,256]{2,1,0:T(8,128)}, u32[]{:S(2)}) copy-start(s32[2,8,256]{2,1,0:T(8,128)} %param.25) | copy-start | bytes 49156
  14.6 10.8 %collective-permute-start = (f32[16,3,1,8,256]{4,3,2,1,0:T(8,128)S(1)}, f32[16,3,1,8,256]{4,3,2,1,0:T(8,128)S(1)}, u32[]{:S(2)}, u32[]{:S(2)}) collective-permute-start(f32[16,3,1,8,256]{4,3,2,1,0:T(8,128)S(1)} %slice.472), channel_id=1, source_target_pairs={{4,0},{8,4},{12,8},{16,12},{20,16},{24,20},{28,24},{32,28},{36,32}... | collective-permute-start | bytes 1179656 | tf_op jit(solution)/shard_map/ppermute | solution.py:19
  20.9 4.6 %copy-start = (f32[8,3,8,3,1,1]{2,0,3,1,5,4:T(8,128)S(1)}, f32[8,3,8,3,1,1]{2,0,3,1,5,4:T(8,128)}, u32[]{:S(2)}) copy-start(f32[8,3,8,3,1,1]{2,0,3,1,5,4:T(8,128)} %constant.380) | copy-start | bytes 6916
  81.2 6.6 %collective-permute-start.1 = (f32[16,3,1,8,256]{4,3,2,1,0:T(8,128)S(1)}, f32[16,3,1,8,256]{4,3,2,1,0:T(8,128)S(1)}, u32[]{:S(2)}, u32[]{:S(2)}) collective-permute-start(f32[16,3,1,8,256]{4,3,2,1,0:T(8,128)S(1)} %slice.399), channel_id=1, source_target_pairs={{0,4},{4,8},{8,12},{12,16},{16,20},{20,24},{24,28},{28,32},{32,36}... | collective-permute-start | bytes 1179656 | tf_op jit(solution)/shard_map/ppermute | solution.py:19
